TPU v7x, 256 devices: a whole 4x4x8 slice. The times are simulated.
256 devices in a mesh: wide: 64 (over y, z, core), narrow: 4 (over x).
Axes of the slice: x: 4, y: 4, z: 8, core: 2. Of those that a mesh axis runs over, the one named last changes fastest.
Arguments:
- features: bfloat16 [768, 524288], P('narrow', 'wide'), may hold values from -6 to 6
- owner_of: int32 [32768, 16, 1], P('wide'), may hold values from 0 to 63; in each aligned block of 8192 rows (0 to 8191, 8192 to 16383, ..., all dimensions but the last counted through in order) at most 192 rows name the same one
- row_of: int32 [32768, 16], P('wide'), may hold values from 0 to 8191
- w_self: bfloat16 [768, 256], P('narrow'), may hold values from -0.15625 to 0.15625
- w_neighbor: bfloat16 [768, 256], P('narrow'), may hold values from -0.15625 to 0.15625
- cotangent: bfloat16 [32768, 256], P(('wide', 'narrow')), may hold values from -0.032958984 to 0.032958984
Outputs:
- hidden: bfloat16 [32768, 256], P(('wide', 'narrow'))
- grad_self: float32 [768, 256], P('narrow')
- grad_neighbor: float32 [768, 256], P('narrow')
Inputs may be any that keep to these rules, and one draw needn't show every extreme that they name: `owner_of`: among the 8192 rows read by the targets of one index of wide, no owner is named more than 192 times, and in every draw some owner is named exactly 192 times by some index.
All inputs are finite; a program needn't handle non-finite values.
Results may differ from a plain program's by a relative error of at most 0.0054.
Values may be sent and summed in bfloat16 or wider, within the bound.
A program may use at most 64 MiB of HBM per device.

v0:
```python
import jax
import jax.numpy as jnp
from jax import lax
from jax.sharding import PartitionSpec as P

FANOUT = 15


def activation(value):
    return jax.nn.gelu(value, approximate=True)


def contract_rows(left, right):
    return lax.dot_general(
        left, right, (((0,), (0,)), ((), ())), preferred_element_type=jnp.float32
    )


def slot_numbers(owners, wide_count, total):
    block_rows = 128
    block_count = total // block_rows
    onehot = (owners[:, None] == jnp.arange(wide_count, dtype=jnp.int32)[None, :]).astype(
        jnp.float32
    )
    blocked = onehot.reshape(block_count, block_rows, wide_count)
    lower = (jnp.arange(block_rows)[:, None] > jnp.arange(block_rows)[None, :]).astype(jnp.float32)
    within = jnp.einsum("ij,bjw->biw", lower, blocked, precision=lax.Precision.HIGHEST)
    block_sums = jnp.sum(blocked, axis=1)
    offsets = jnp.cumsum(block_sums, axis=0) - block_sums
    prefix = within + offsets[:, None, :]
    return jnp.sum(prefix * blocked, axis=2).reshape(total).astype(jnp.int32)


def on_device(features, owner_of, row_of, w_self, w_neighbor, cotangent):
    wide_count = lax.axis_size("wide")
    narrow_count = lax.axis_size("narrow")
    tgt_rows, request_count = row_of.shape
    feat_cols = features.shape[0]
    total = tgt_rows * request_count
    capacity = max(2, 3 * total // (2 * wide_count))
    owners = owner_of.reshape(total)
    wanted = row_of.reshape(total)
    slot_of = slot_numbers(owners, wide_count, total)
    flat_slot = owners * capacity + slot_of
    buffer = (
        jnp.zeros((wide_count * capacity,), jnp.int32)
        .at[flat_slot]
        .set(wanted)
        .reshape(wide_count, capacity)
    )
    table = jnp.transpose(features)
    found = jnp.take(
        table, lax.all_to_all(buffer, "wide", split_axis=0, concat_axis=0, tiled=True), axis=0
    )
    fetched = lax.all_to_all(found, "wide", split_axis=0, concat_axis=0, tiled=True)
    flat_fetched = fetched.reshape(wide_count * capacity, feat_cols)
    gathered = jnp.take(flat_fetched, flat_slot, axis=0).reshape(tgt_rows, request_count, feat_cols)
    self_rows = gathered[:, 0]
    pooled = (jnp.sum(gathered[:, 1:], axis=1, dtype=jnp.float32) / FANOUT).astype(jnp.bfloat16)
    share = tgt_rows // narrow_count
    preact = lax.psum(
        jnp.dot(self_rows, w_self, preferred_element_type=jnp.float32)
        + jnp.dot(pooled, w_neighbor, preferred_element_type=jnp.float32),
        "narrow",
    )
    value, pullback = jax.vjp(activation, preact)
    full_cot = lax.all_gather(cotangent, "narrow", axis=0, tiled=True)
    slope = pullback(full_cot.astype(jnp.float32))[0].astype(jnp.bfloat16)
    mine = lax.axis_index("narrow") * share
    hidden = lax.dynamic_slice_in_dim(value, mine, share, 0).astype(jnp.bfloat16)
    grad_self, grad_neighbor = lax.psum(
        (contract_rows(self_rows, slope), contract_rows(pooled, slope)), "wide"
    )
    return (hidden, grad_self, grad_neighbor)


def solution(mesh):
    return jax.shard_map(
        on_device,
        mesh=mesh,
        in_specs=(
            P("narrow", "wide"),
            P("wide", None, None),
            P("wide", None),
            P("narrow", None),
            P("narrow", None),
            P(("wide", "narrow"), None),
        ),
        out_specs=(P(("wide", "narrow"), None), P("narrow", None), P("narrow", None)),
        check_vma=False,
    )
```

profile of v0, /device:TPU:2, one launch (start us, length us, event | category | flops | bytes accessed | tf_op | source)
XLA Modules:
  0.0 561.9 jit_solution(12965184154446572540)
XLA Ops:
  7.2 1.0 copy.24
  8.2 1.4 copy_multiply_fusion
  11.3 0.9 copy.26
  15.4 30.7 %scatter_custom_fusion = s32[12288]{0:T(1024)S(1)} fusion(s32[8192]{0:T(1024)S(1)} %bitcast.41, s32[8192]{0:T(1024)} %reshape.155, s32[]{:T(128)} %constant.21.clone.1), kind=kCustom, calls=%fused_computation.47 | custom fusion | bytes 49664 | tf_op jit(solution)/shard_map/scatter | solution.py:48
  46.9 12.1 %all-to-all-start = ((s32[64,1,192]{2,1,0:T(1,128)}), s32[64,1,192]{2,1,0:T(1,128)S(1)}, u32[]{:S(2)}, u32[]{:S(2)}) async-start(s32[64,1,192]{2,1,0:T(1,128)} %all_to_all.13), calls=%async_computation | async-start | bytes 131072 | tf_op jit(solution)/shard_map/all_to_all | solution.py:53
  59.0 4.0 copy.28
  63.0 5.7 %all-to-all-done = s32[64,1,192]{2,1,0:T(1,128)S(1)} async-done(((s32[64,1,192]{2,1,0:T(1,128)}), s32[64,1,192]{2,1,0:T(1,128)S(1)}, u32[]{:S(2)}, u32[]{:S(2)}) %all-to-all-start) | async-done | bytes 49184 | tf_op jit(solution)/shard_map/all_to_all | solution.py:53
  69.0 48.5 %gather_fusion = bf16[12288,192]{1,0:T(8,128)(2,1)} fusion(bf16[8192,192]{1,0:T(8,128)(2,1)} %bitcast.37, s32[12288]{0:T(1024)S(1)} %broadcast_clamp_fusion), kind=kCustom, calls=%fused_computation | custom fusion | bytes 9486336 | tf_op jit(solution)/shard_map/jit(_take)/gather | solution.py:52
  117.6 7.6 %broadcast_select_fusion = bf16[64,192,192]{2,1,0:T(8,128)(2,1)} fusion(bf16[64,192,192]{2,1,0:T(8,128)(2,1)} %bitcast.38, pred[64,192]{1,0:T(8,128)(4,1)S(1)} %compare_and_fusion), kind=kLoop, calls=%fused_computation.3 | loop fusion | flops 2359296 | bytes 9449472 | tf_op jit(solution)/shard_map/jit(_take)/select_n | solution.py:52
  125.2 5.8 %all-to-all-start.1 = ((bf16[64,192,192]{2,1,0:T(8,128)(2,1)}), bf16[64,192,192]{2,1,0:T(8,128)(2,1)}, u32[]{:S(2)}, u32[]{:S(2)}) async-start(bf16[64,192,192]{2,1,0:T(8,128)(2,1)} %broadcast_select_fusion), calls=%async_computation.1 | async-start | bytes 12582912 | tf_op jit(solution)/shard_map/all_to_all | solution.py:55
  131.4 139.8 %all-to-all-done.1 = bf16[64,192,192]{2,1,0:T(8,128)(2,1)} async-done(((bf16[64,192,192]{2,1,0:T(8,128)(2,1)}), bf16[64,192,192]{2,1,0:T(8,128)(2,1)}, u32[]{:S(2)}, u32[]{:S(2)}) %all-to-all-start.1) | async-done | bytes 4718624 | tf_op jit(solution)/shard_map/all_to_all | solution.py:55
  271.2 34.5 %gather_fusion.1 = bf16[8192,192]{1,0:T(8,128)(2,1)} fusion(bf16[12288,192]{1,0:T(8,128)(2,1)} %bitcast.8, s32[8192]{0:T(1024)S(1)} %broadcast_clamp_fusion.1), kind=kCustom, calls=%fused_computation.1 | custom fusion | bytes 6324224 | tf_op jit(solution)/shard_map/jit(_take)/gather | solution.py:57
  305.7 7.7 %copy.29 = bf16[512,16,192]{0,2,1:T(8,128)(2,1)} copy(bf16[512,16,192]{2,1,0:T(8,128)(2,1)} %bitcast.39) | data formatting | bytes 6291456 | tf_op jit(solution)/shard_map/jit(_take)/gather | solution.py:57
  313.4 2.2 broadcast_select_fusion.1
  316.8 1.1 convolution_add_fusion
  317.9 12.5 %all_gather.3 = bf16[512,256]{1,0:T(8,128)(2,1)S(1)} all-gather(bf16[128,256]{1,0:T(8,128)(2,1)} %param.11), channel_id=1, replica_groups=mesh['wide'=64,'narrow'=4] {'narrow'}, dimensions={0}, use_global_device_ids=true | all-gather | bytes 327680 | tf_op jit(solution)/shard_map/all_gather | solution.py:67
  330.5 32.0 %all-reduce.4.cloned.1.call-done = f32[512,256]{1,0:T(8,128)} async-done(((f32[512,256]{1,0:T(8,128)}), f32[512,256]{1,0:T(8,128)}) %all-reduce.4.cloned.1.call-update) | async-done | bytes 524304 | tf_op jit(solution)/shard_map/psum | solution.py:61
  362.5 2.2 fusion.5
  364.7 1.9 fusion.16
  366.6 0.9 fusion.13
  367.5 1.6 fusion.15
  369.1 182.7 %all-reduce.6.cloned.1.call-done = (f32[192,256]{1,0:T(8,128)}, f32[192,256]{1,0:T(8,128)}) async-done(((f32[192,256]{1,0:T(8,128)}, f32[192,256]{1,0:T(8,128)}), (f32[192,256]{1,0:T(8,128)}, f32[192,256]{1,0:T(8,128)})) %all-reduce.6.cloned.1.call-update) | async-done | bytes 393232 | tf_op jit(solution)/shard_map/psum | solution.py:71
  551.9 1.6 copy.40
  553.5 1.6 copy.41
  (35 shorter events, 7.5 us)
Async XLA Ops:
  7.2 308.9 %copy-start = (bf16[192,256]{1,0:T(8,128)(2,1)S(1)}, bf16[192,256]{1,0:T(8,128)(2,1)}, u32[]{:S(2)}) copy-start(bf16[192,256]{1,0:T(8,128)(2,1)} %param.9) | copy-start | bytes 294916
  7.2 51.8 %copy-start.2 = (bf16[192,8192]{1,0:T(8,128)(2,1)S(1)}, bf16[192,8192]{1,0:T(8,128)(2,1)}, u32[]{:S(2)}) copy-start(bf16[192,8192]{1,0:T(8,128)(2,1)} %param.6) | copy-start | bytes 9437188
  46.9 21.8 %all-to-all-start = ((s32[64,1,192]{2,1,0:T(1,128)}), s32[64,1,192]{2,1,0:T(1,128)S(1)}, u32[]{:S(2)}, u32[]{:S(2)}) async-start(s32[64,1,192]{2,1,0:T(1,128)} %all_to_all.13), calls=%async_computation | async-start | bytes 131072 | tf_op jit(solution)/shard_map/all_to_all | solution.py:53
  125.2 6.1 %copy-start.3 = (s32[512,16,1]{0,2,1:T(1,128)S(1)}, s32[512,16,1]{0,2,1:T(1,128)}, u32[]{:S(2)}) copy-start(s32[512,16,1]{0,2,1:T(1,128)} %param.7) | copy-start | bytes 98308
  125.2 146.0 %all-to-all-start.1 = ((bf16[64,192,192]{2,1,0:T(8,128)(2,1)}), bf16[64,192,192]{2,1,0:T(8,128)(2,1)}, u32[]{:S(2)}, u32[]{:S(2)}) async-start(bf16[64,192,192]{2,1,0:T(8,128)(2,1)} %broadcast_select_fusion), calls=%async_computation.1 | async-start | bytes 12582912 | tf_op jit(solution)/shard_map/all_to_all | solution.py:55
  131.0 231.5 %all-reduce.4.cloned.1.call-start = ((), (), s32[]{:S(2)}) async-start(), calls=%async_computation.2 | async-start | bytes 1048576 | tf_op jit(solution)/shard_map/psum | solution.py:61
  315.6 1.2 copy-start.4
  316.0 0.7 copy-start.1
  317.9 234.0 %all-reduce.6.cloned.1.call-start = ((), (), s32[]{:S(2)}) async-start(), calls=%async_computation.3 | async-start | bytes 786432 | tf_op jit(solution)/shard_map/psum | solution.py:71
Sparse Core Ops, SparseCore 0:
  318.0 44.4 all-reduce.3
  367.6 184.1 all-reduce.5
where the time goes:
time: 563 us; the launch traced here: 562 us
  waiting for transfers between devices  360 us (64%)
  local copies, waits for them, and re-layouts  135 us (24%)
  starting transfers between devices  18 us (3%)
  other arithmetic  17.3 us (3%)
  between operations  14.2 us (3%)
  blocking collectives  12.5 us (2%)
    psum x1, waiting for transfers between devices, on_device(): lax.psum((contract_rows(self_rows, slope), contract_rows(pooled, slope)),...  183 us
    all_to_all x1, waiting for transfers between devices, on_device(): lax.all_to_all(found, 'wide', split_axis=0, concat_axis=0, tiled=True)  140 us
    gather x1, local copies, waits for them, and re-layouts, on_device(): jnp.take(table, lax.all_to_all(buffer, 'wide', split_axis=0, concat_axis=...  48.5 us
    gather x2, local copies, waits for them, and re-layouts, on_device(): jnp.take(flat_fetched, flat_slot, axis=0)  42.2 us
    psum x1, waiting for transfers between devices, on_device(): lax.psum(jnp.dot(self_rows, w_self, preferred_element_type=jnp.float32) +...  32 us
    scatter x1, local copies, waits for them, and re-layouts, on_device(): buffer = jnp.zeros((wide_count * capacity,), jnp.int32).at[flat_slot].set...  30.7 us
    all_gather x1, blocking collectives, on_device(): full_cot = lax.all_gather(cotangent, 'narrow', axis=0, tiled=True)  12.5 us
    all_to_all x1, starting transfers between devices, on_device(): lax.all_to_all(buffer, 'wide', split_axis=0, concat_axis=0, tiled=True)  12.1 us
  transfers between devices with their start and end apart: 4, of which 4 were waited for; matrix products, arithmetic and copies ran while one was open for 1% of the time, Pallas kernels for 0%

commit v1 on v0

--- a/solution.py
+++ b/solution.py
@@ -4,6 +4,10 @@
 from jax.sharding import PartitionSpec as P
 
 FANOUT = 15
+
+
+def _attach_corner(frame, lane_axis):
+    return jax.lax.all_gather(frame, axis_name=lane_axis).sum(axis=0)
 
 
 def activation(value):
@@ -58,7 +62,7 @@
     self_rows = gathered[:, 0]
     pooled = (jnp.sum(gathered[:, 1:], axis=1, dtype=jnp.float32) / FANOUT).astype(jnp.bfloat16)
     share = tgt_rows // narrow_count
-    preact = lax.psum(
+    preact = _attach_corner(
         jnp.dot(self_rows, w_self, preferred_element_type=jnp.float32)
         + jnp.dot(pooled, w_neighbor, preferred_element_type=jnp.float32),
         "narrow",

time: 563 us -> 550 us (0.977)
  waiting for transfers between devices: 360 us -> 344 us
    psum x1 -> x0, waiting for transfers between devices: 32 us -> none  [on_device(): lax.psum(jnp.dot(self_rows, w_self, preferred_element_type=jnp.float32) +...]
    all_gather x0 -> x1, waiting for transfers between devices: none -> 16.7 us  [_attach_corner(): return jax.lax.all_gather(frame, axis_name=lane_axis).sum(axis=0)]
where the time goes in v1:
time: 550 us; the launch traced here: 549 us
  waiting for transfers between devices  344 us (63%)
  local copies, waits for them, and re-layouts  135 us (25%)
  other arithmetic  19.8 us (4%)
  starting transfers between devices  18 us (3%)
  between operations  14.2 us (3%)
  blocking collectives  13 us (2%)
    psum x1, waiting for transfers between devices, on_device(): lax.psum((contract_rows(self_rows, slope), contract_rows(pooled, slope)),...  182 us
    all_to_all x1, waiting for transfers between devices, on_device(): lax.all_to_all(found, 'wide', split_axis=0, concat_axis=0, tiled=True)  140 us
    gather x1, local copies, waits for them, and re-layouts, on_device(): jnp.take(table, lax.all_to_all(buffer, 'wide', split_axis=0, concat_axis=...  48.5 us
    gather x2, local copies, waits for them, and re-layouts, on_device(): jnp.take(flat_fetched, flat_slot, axis=0)  42.2 us
    scatter x1, local copies, waits for them, and re-layouts, on_device(): buffer = jnp.zeros((wide_count * capacity,), jnp.int32).at[flat_slot].set...  30.7 us
    all_gather x1, waiting for transfers between devices, _attach_corner(): return jax.lax.all_gather(frame, axis_name=lane_axis).sum(axis=0)  16.7 us
    all_gather x1, blocking collectives, on_device(): full_cot = lax.all_gather(cotangent, 'narrow', axis=0, tiled=True)  13 us
    all_to_all x1, starting transfers between devices, on_device(): lax.all_to_all(buffer, 'wide', split_axis=0, concat_axis=0, tiled=True)  12.1 us
  transfers between devices with their start and end apart: 4, of which 4 were waited for; matrix products, arithmetic and copies ran while one was open for 1% of the time, Pallas kernels for 0%

profile of v1, /device:TPU:2, one launch (start us, length us, event | category | flops | bytes accessed | tf_op | source)
XLA Modules:
  0.0 549.2 jit_solution(1189586559757823041)
XLA Ops:
  7.2 1.0 copy.24
  8.2 1.4 copy_multiply_fusion
  15.4 30.7 %scatter_custom_fusion = s32[12288]{0:T(1024)S(1)} fusion(s32[8192]{0:T(1024)S(1)} %bitcast.43, s32[8192]{0:T(1024)} %reshape.155, s32[]{:T(128)} %constant.21.clone.1), kind=kCustom, calls=%fused_computation.47 | custom fusion | bytes 49664 | tf_op jit(solution)/shard_map/scatter | solution.py:52
  46.9 12.1 %all-to-all-start = ((s32[64,1,192]{2,1,0:T(1,128)}), s32[64,1,192]{2,1,0:T(1,128)S(1)}, u32[]{:S(2)}, u32[]{:S(2)}) async-start(s32[64,1,192]{2,1,0:T(1,128)} %all_to_all.13), calls=%async_computation | async-start | bytes 131072 | tf_op jit(solution)/shard_map/all_to_all | solution.py:57
  59.0 4.0 copy.28
  63.0 5.7 %all-to-all-done = s32[64,1,192]{2,1,0:T(1,128)S(1)} async-done(((s32[64,1,192]{2,1,0:T(1,128)}), s32[64,1,192]{2,1,0:T(1,128)S(1)}, u32[]{:S(2)}, u32[]{:S(2)}) %all-to-all-start) | async-done | bytes 49184 | tf_op jit(solution)/shard_map/all_to_all | solution.py:57
  69.0 48.5 %gather_fusion = bf16[12288,192]{1,0:T(8,128)(2,1)} fusion(bf16[8192,192]{1,0:T(8,128)(2,1)} %bitcast.38, s32[12288]{0:T(1024)S(1)} %broadcast_clamp_fusion), kind=kCustom, calls=%fused_computation | custom fusion | bytes 9486336 | tf_op jit(solution)/shard_map/jit(_take)/gather | solution.py:56
  117.6 7.6 %broadcast_select_fusion = bf16[64,192,192]{2,1,0:T(8,128)(2,1)} fusion(bf16[64,192,192]{2,1,0:T(8,128)(2,1)} %bitcast.39, pred[64,192]{1,0:T(8,128)(4,1)S(1)} %compare_and_fusion), kind=kLoop, calls=%fused_computation.3 | loop fusion | flops 2359296 | bytes 9449472 | tf_op jit(solution)/shard_map/jit(_take)/select_n | solution.py:56
  125.2 5.8 %all-to-all-start.1 = ((bf16[64,192,192]{2,1,0:T(8,128)(2,1)}), bf16[64,192,192]{2,1,0:T(8,128)(2,1)}, u32[]{:S(2)}, u32[]{:S(2)}) async-start(bf16[64,192,192]{2,1,0:T(8,128)(2,1)} %broadcast_select_fusion), calls=%async_computation.1 | async-start | bytes 12582912 | tf_op jit(solution)/shard_map/all_to_all | solution.py:59
  131.4 139.8 %all-to-all-done.1 = bf16[64,192,192]{2,1,0:T(8,128)(2,1)} async-done(((bf16[64,192,192]{2,1,0:T(8,128)(2,1)}), bf16[64,192,192]{2,1,0:T(8,128)(2,1)}, u32[]{:S(2)}, u32[]{:S(2)}) %all-to-all-start.1) | async-done | bytes 4718624 | tf_op jit(solution)/shard_map/all_to_all | solution.py:59
  271.2 34.5 %gather_fusion.1 = bf16[8192,192]{1,0:T(8,128)(2,1)} fusion(bf16[12288,192]{1,0:T(8,128)(2,1)} %bitcast.8, s32[8192]{0:T(1024)S(1)} %broadcast_clamp_fusion.1), kind=kCustom, calls=%fused_computation.1 | custom fusion | bytes 6324224 | tf_op jit(solution)/shard_map/jit(_take)/gather | solution.py:61
  305.7 7.7 %copy.29 = bf16[512,16,192]{0,2,1:T(8,128)(2,1)} copy(bf16[512,16,192]{2,1,0:T(8,128)(2,1)} %bitcast.40) | data formatting | bytes 6291456 | tf_op jit(solution)/shard_map/jit(_take)/gather | solution.py:61
  313.4 2.2 broadcast_select_fusion.1
  316.8 1.1 convolution_add_fusion
  317.9 13.0 %all_gather.11 = bf16[512,256]{1,0:T(8,128)(2,1)S(1)} all-gather(bf16[128,256]{1,0:T(8,128)(2,1)} %param.11), channel_id=1, replica_groups=mesh['wide'=64,'narrow'=4] {'narrow'}, dimensions={0}, use_global_device_ids=true | all-gather | bytes 327680 | tf_op jit(solution)/shard_map/all_gather | solution.py:71
  331.0 16.7 %all-gather.3.cloned.1.call-done = f32[2048,256]{1,0:T(8,128)} async-done(((f32[512,256]{1,0:T(8,128)}), f32[2048,256]{1,0:T(8,128)}) %all-gather.3.cloned.1.call-update) | async-done | bytes 2097168 | tf_op jit(solution)/shard_map/all_gather | solution.py:10
  347.7 2.6 reduce_sum.39
  350.2 2.2 fusion.5
  352.5 1.9 fusion.16
  354.3 0.9 fusion.13
  355.3 1.6 fusion.15
  356.9 182.2 %all-reduce.3.cloned.1.call-done = (f32[192,256]{1,0:T(8,128)}, f32[192,256]{1,0:T(8,128)}) async-done(((f32[192,256]{1,0:T(8,128)}, f32[192,256]{1,0:T(8,128)}), (f32[192,256]{1,0:T(8,128)}, f32[192,256]{1,0:T(8,128)})) %all-reduce.3.cloned.1.call-update) | async-done | bytes 393232 | tf_op jit(solution)/shard_map/psum | solution.py:75
  539.1 1.6 copy.39
  540.7 1.6 copy.40
  (36 shorter events, 8.4 us)
Async XLA Ops:
  7.2 308.9 %copy-start = (bf16[192,256]{1,0:T(8,128)(2,1)S(1)}, bf16[192,256]{1,0:T(8,128)(2,1)}, u32[]{:S(2)}) copy-start(bf16[192,256]{1,0:T(8,128)(2,1)} %param.9) | copy-start | bytes 294916
  7.2 51.8 %copy-start.2 = (bf16[192,8192]{1,0:T(8,128)(2,1)S(1)}, bf16[192,8192]{1,0:T(8,128)(2,1)}, u32[]{:S(2)}) copy-start(bf16[192,8192]{1,0:T(8,128)(2,1)} %param.6) | copy-start | bytes 9437188
  46.9 21.8 %all-to-all-start = ((s32[64,1,192]{2,1,0:T(1,128)}), s32[64,1,192]{2,1,0:T(1,128)S(1)}, u32[]{:S(2)}, u32[]{:S(2)}) async-start(s32[64,1,192]{2,1,0:T(1,128)} %all_to_all.13), calls=%async_computation | async-start | bytes 131072 | tf_op jit(solution)/shard_map/all_to_all | solution.py:57
  125.2 6.1 %copy-start.3 = (s32[512,16,1]{0,2,1:T(1,128)S(1)}, s32[512,16,1]{0,2,1:T(1,128)}, u32[]{:S(2)}) copy-start(s32[512,16,1]{0,2,1:T(1,128)} %param.7) | copy-start | bytes 98308
  125.2 146.0 %all-to-all-start.1 = ((bf16[64,192,192]{2,1,0:T(8,128)(2,1)}), bf16[64,192,192]{2,1,0:T(8,128)(2,1)}, u32[]{:S(2)}, u32[]{:S(2)}) async-start(bf16[64,192,192]{2,1,0:T(8,128)(2,1)} %broadcast_select_fusion), calls=%async_computation.1 | async-start | bytes 12582912 | tf_op jit(solution)/shard_map/all_to_all | solution.py:59
  131.0 216.6 %all-gather.3.cloned.1.call-start = ((), (), s32[]{:S(2)}) async-start(), calls=%async_computation.2 | async-start | bytes 2621440 | tf_op jit(solution)/shard_map/all_gather | solution.py:10
  315.6 1.2 copy-start.4
  316.0 0.7 copy-start.1
  317.9 221.2 %all-reduce.3.cloned.1.call-start = ((), (), s32[]{:S(2)}) async-start(), calls=%async_computation.3 | async-start | bytes 786432 | tf_op jit(solution)/shard_map/psum | solution.py:75
Sparse Core Ops, SparseCore 0:
  318.0 29.6 all-gather.2
  355.4 183.6 all-reduce.2
